TPU v7x, 32 devices: a whole 2x2x4 slice. The times are simulated.
32 devices in a mesh: sect: 4 (over y, x), tile: 8 (over z, core).
Axes of the slice: x: 2, y: 2, z: 4, core: 2. Of those that a mesh axis runs over, the one named last changes fastest.
Arguments:
- zonal: float32 [4, 64, 512], P('sect', 'tile'), may hold values from -1.5 to 1.5
- merid: float32 [4, 64, 512], P('sect', 'tile'), may hold values from -1.5 to 1.5
- height: float32 [4, 64, 512], P('sect', 'tile'), may hold values from -6 to 6
- level_kappa: float32 [4], replicated, may hold values from 0.2 to 2
- sea: int32 [64, 512], P('tile'), may hold values 0 or 1
- flags: int32 [4, 64, 512], P(None, 'tile', 'sect'), may hold values 0 or 1
- conc: float32 [12, 4, 64, 512], P(None, None, 'tile', 'sect'), may hold values from 0.1 to 2
- react: float32 [12, 12], replicated, may hold values from -1.2 to 1.2
- absorb: float32 [12], replicated, may hold values from 0.05 to 1
- light: float32 [4], replicated, may hold values from 0.1 to 1
Outputs:
- conc_out: float32 [12, 4, 64, 512], P(None, None, 'tile', 'sect')
- zonal_out: float32 [4, 64, 512], P('sect', 'tile')
- merid_out: float32 [4, 64, 512], P('sect', 'tile')
- height_out: float32 [4, 64, 512], P('sect', 'tile')
All inputs are finite; a program needn't handle non-finite values. No bound on the sum of `sea` or of `flags` on one device may be relied on, other than what follows from the above.
Results may differ from a plain program's by a relative error of at most 0.00022.
Values sent between devices are 32-bit elements; how exact they have to be, the bound alone decides.
A program may use at most 64 MiB of HBM per device.

v0:
```python
import jax
import jax.numpy as jnp
from jax import lax
from jax.sharding import PartitionSpec as P

STEPS = 4
INTERVALS = 2
time_step = 0.1
gravity = 1.0
coriolis = 0.3
viscosity = 0.05
heat_coupling = 0.05
tracer_step = 0.5
stir_gain = 4.0


def padded_2(cells, sides, width):
    for axis, dim in sides:
        count = lax.axis_size(axis)
        head = lax.slice_in_dim(cells, 0, width, axis=dim)
        tail = lax.slice_in_dim(cells, cells.shape[dim] - width, cells.shape[dim], axis=dim)
        cells = jnp.concatenate(
            [
                lax.ppermute(tail, axis, [(i, (i + 1) % count) for i in range(count)]),
                cells,
                lax.ppermute(head, axis, [((i + 1) % count, i) for i in range(count)]),
            ],
            axis=dim,
        )
    return cells


def along_x(field):
    return 0.5 * (jnp.roll(field, -1, 2) - jnp.roll(field, 1, 2))


def along_y(padded):
    return 0.5 * (padded[:, 2:] - padded[:, :-2])


def laplace(field, padded):
    total = padded[:, 2:] + padded[:, :-2]
    total = total + jnp.roll(field, -1, 2) + jnp.roll(field, 1, 2)
    return total - 4.0 * field


def upwind(centre, ahead, behind, speed, flag):
    upper = jnp.maximum(speed, 0.0) * (centre - behind) + jnp.minimum(speed, 0.0) * (ahead - centre)
    middle = 0.5 * speed * (ahead - behind)
    return jnp.where(flag == 1, upper, middle)


def column_solve(starred, kappa):
    levels = starred.shape[1]
    couple = [tracer_step * 0.5 * (kappa[k] + kappa[k + 1]) for k in range(levels - 1)]
    factor = []
    partial_rhs = []
    for k in range(levels):
        lower = couple[k - 1] if k > 0 else jnp.zeros_like(kappa[0])
        upper = couple[k] if k < levels - 1 else jnp.zeros_like(kappa[0])
        diagonal = 1.0 + lower + upper
        if k == 0:
            denom = diagonal
            rhs_now = starred[:, 0] / denom
        else:
            denom = diagonal + lower * factor[k - 1]
            rhs_now = (starred[:, k] + lower * partial_rhs[k - 1]) / denom
        factor.append(-upper / denom)
        partial_rhs.append(rhs_now)
    result = [None] * levels
    result[levels - 1] = partial_rhs[levels - 1]
    for k in range(levels - 2, -1, -1):
        result[k] = partial_rhs[k] - factor[k] * result[k + 1]
    return jnp.stack(result, axis=1)


def body(zonal, merid, height, level_kappa, sea, flags, conc, react, absorb, light):
    sect_index = lax.axis_index("sect")
    levels_dev = zonal.shape[0]
    column_dev = conc.shape[3]
    wet_rows = sea.astype(jnp.float32)
    wet_cols = lax.dynamic_slice_in_dim(wet_rows, sect_index * column_dev, column_dev, 1)
    own_kappa = lax.dynamic_slice_in_dim(level_kappa, sect_index * levels_dev, levels_dev, 0)
    forcing = jnp.zeros(height.shape, jnp.float32)
    for interval in range(INTERVALS):
        zonal_sum = jnp.zeros(zonal.shape, jnp.float32)
        merid_sum = jnp.zeros(merid.shape, jnp.float32)
        for step in range(STEPS):
            forced = height + time_step * heat_coupling * forcing
            wide = padded_2(jnp.stack([zonal, merid, forced]), (("tile", 2),), 2)
            zonal_wide = wide[0]
            merid_wide = wide[1]
            forced_wide = wide[2]
            zonal_pad = zonal_wide[:, 1:-1]
            merid_pad = merid_wide[:, 1:-1]
            height_ext = forced_wide[:, 1:-1] - time_step * (
                along_x(zonal_pad) + along_y(merid_wide)
            )
            height = height_ext[:, 1:-1]
            zonal_new = wet_rows * (
                zonal
                + time_step
                * (
                    coriolis * merid
                    - gravity * along_x(height)
                    + viscosity * laplace(zonal, zonal_pad)
                )
            )
            merid_new = wet_rows * (
                merid
                + time_step
                * (
                    -coriolis * zonal
                    - gravity * along_y(height_ext)
                    + viscosity * laplace(merid, merid_pad)
                )
            )
            zonal, merid = (zonal_new, merid_new)
            zonal_sum = zonal_sum + zonal
            merid_sum = merid_sum + merid
        zonal_mean = zonal_sum / STEPS
        merid_mean = merid_sum / STEPS
        kappa_rows = own_kappa[:, None, None] * (
            1.0 + stir_gain * (zonal_mean * zonal_mean + merid_mean * merid_mean)
        )
        arrived = lax.all_to_all(
            jnp.stack([zonal_mean, merid_mean, kappa_rows]),
            "sect",
            split_axis=3,
            concat_axis=1,
            tiled=True,
        )
        zonal_cols = arrived[0]
        merid_cols = arrived[1]
        kappa_cols = arrived[2]
        padded = padded_2(conc, (("tile", 2), ("sect", 3)), 1)
        east = padded[:, :, 1:-1, 2:]
        west = padded[:, :, 1:-1, :-2]
        north = padded[:, :, 2:, 1:-1]
        south = padded[:, :, :-2, 1:-1]
        moving_terms = upwind(conc, east, west, zonal_cols, flags) + upwind(
            conc, north, south, merid_cols, flags
        )
        starred = conc - tracer_step * wet_cols * moving_terms
        mixed = column_solve(starred, kappa_cols)
        growth = jnp.einsum("ij,jzyx->izyx", react, mixed, precision=lax.Precision.HIGHEST)
        conc = mixed + tracer_step * wet_cols * growth
        if interval + 1 < INTERVALS:
            heat_cols = light[:, None, None] * jnp.einsum(
                "k,kzyx->zyx", absorb, conc, precision=lax.Precision.HIGHEST
            )
            forcing = lax.all_to_all(heat_cols, "sect", split_axis=0, concat_axis=2, tiled=True)
    return (conc, zonal, merid, height)


def solution(mesh):
    placed = (
        P("sect", "tile", None),
        P("sect", "tile", None),
        P("sect", "tile", None),
        P(),
        P("tile", None),
        P(None, "tile", "sect"),
        P(None, None, "tile", "sect"),
        P(),
        P(),
        P(),
    )
    return jax.shard_map(
        body,
        mesh=mesh,
        in_specs=placed,
        out_specs=(
            P(None, None, "tile", "sect"),
            P("sect", "tile", None),
            P("sect", "tile", None),
            P("sect", "tile", None),
        ),
        check_vma=False,
    )
```

profile of v0, /device:TPU:0, one launch (start us, length us, event | category | flops | bytes accessed | tf_op | source)
XLA Modules:
  0.0 116.7 jit_solution(4213536475629891333)
XLA Ops:
  0.6 0.8 pad_maximum_fusion.46
  2.0 4.1 %collective-permute-start.1 = (f32[3,1,2,512]{3,2,1,0:T(2,128)S(1)}, f32[3,1,2,512]{3,2,1,0:T(2,128)S(1)}, u32[]{:S(2)}, u32[]{:S(2)}) collective-permute-start(f32[3,1,2,512]{3,2,1,0:T(2,128)S(1)} %get-tuple-element.119), channel_id=1, source_target_pairs={{1,0},{2,1},{3,2},{4,3},{5,4},{6,5},{7,6},{0,7},{9,8},{10,9},{11,1... | collective-permute-start | bytes 36872 | tf_op jit(solution)/shard_map/ppermute | solution.py:26
  6.1 1.0 copy.503
  7.2 3.5 %collective-permute-start.9 = (f32[12,4,1,128]{3,0,2,1:T(8,128)S(1)}, f32[12,4,1,128]{3,0,2,1:T(8,128)S(1)}, u32[]{:S(2)}, u32[]{:S(2)}) collective-permute-start(f32[12,4,1,128]{3,0,2,1:T(8,128)S(1)} %get-tuple-element.67), channel_id=1, source_target_pairs={{1,0},{2,1},{3,2},{4,3},{5,4},{6,5},{7,6},{0,7},{9,8},{10,9},{11,1... | collective-permute-start | bytes 73736 | tf_op jit(solution)/shard_map/ppermute | solution.py:26
  12.4 0.7 copy-done.8
  15.4 3.5 %collective-permute-start.3 = (f32[3,1,2,512]{3,2,1,0:T(2,128)S(1)}, f32[3,1,2,512]{3,2,1,0:T(2,128)S(1)}, u32[]{:S(2)}, u32[]{:S(2)}) collective-permute-start(f32[3,1,2,512]{3,2,1,0:T(2,128)S(1)} %get-tuple-element.117), channel_id=1, source_target_pairs={{1,0},{2,1},{3,2},{4,3},{5,4},{6,5},{7,6},{0,7},{9,8},{10,9},{11,1... | collective-permute-start | bytes 36872 | tf_op jit(solution)/shard_map/ppermute | solution.py:26
  19.0 1.3 %collective-permute-done.2 = f32[3,1,2,512]{3,2,1,0:T(2,128)S(1)} collective-permute-done((f32[3,1,2,512]{3,2,1,0:T(2,128)S(1)}, f32[3,1,2,512]{3,2,1,0:T(2,128)S(1)}, u32[]{:S(2)}, u32[]{:S(2)}) %collective-permute-start.2) | collective-permute-done | bytes 12320 | tf_op jit(solution)/shard_map/ppermute | solution.py:24
  21.2 3.6 %collective-permute-start.5 = (f32[3,1,2,512]{3,2,1,0:T(2,128)S(1)}, f32[3,1,2,512]{3,2,1,0:T(2,128)S(1)}, u32[]{:S(2)}, u32[]{:S(2)}) collective-permute-start(f32[3,1,2,512]{3,2,1,0:T(2,128)S(1)} %get-tuple-element.115), channel_id=1, source_target_pairs={{1,0},{2,1},{3,2},{4,3},{5,4},{6,5},{7,6},{0,7},{9,8},{10,9},{11,1... | collective-permute-start | bytes 36872 | tf_op jit(solution)/shard_map/ppermute | solution.py:26
  25.6 0.9 fusion.259
  26.5 1.9 %collective-permute-start.10 = (f32[12,4,10,1]{3,0,2,1:T(8,128)}, f32[12,4,10,1]{3,0,2,1:T(8,128)S(1)}, u32[]{:S(2)}, u32[]{:S(2)}) collective-permute-start(f32[12,4,10,1]{3,0,2,1:T(8,128)} %get-tuple-element.62), channel_id=1, source_target_pairs={{0,8},{8,16},{16,24},{24,0},{1,9},{9,17},{17,25},{25,1},{2,10},{10... | collective-permute-start | bytes 5768 | tf_op jit(solution)/shard_map/ppermute | solution.py:24
  28.5 1.0 collective-permute-start.11
  30.2 3.5 %collective-permute-start.7 = (f32[3,1,2,512]{3,2,1,0:T(2,128)S(1)}, f32[3,1,2,512]{3,2,1,0:T(2,128)S(1)}, u32[]{:S(2)}, u32[]{:S(2)}) collective-permute-start(f32[3,1,2,512]{3,2,1,0:T(2,128)S(1)} %get-tuple-element.113), channel_id=1, source_target_pairs={{1,0},{2,1},{3,2},{4,3},{5,4},{6,5},{7,6},{0,7},{9,8},{10,9},{11,1... | collective-permute-start | bytes 36872 | tf_op jit(solution)/shard_map/ppermute | solution.py:26
  33.8 1.3 %collective-permute-done.6 = f32[3,1,2,512]{3,2,1,0:T(2,128)S(1)} collective-permute-done((f32[3,1,2,512]{3,2,1,0:T(2,128)S(1)}, f32[3,1,2,512]{3,2,1,0:T(2,128)S(1)}, u32[]{:S(2)}, u32[]{:S(2)}) %collective-permute-start.6) | collective-permute-done | bytes 12320 | tf_op jit(solution)/shard_map/ppermute | solution.py:24
  35.6 0.8 multiply_bitcast_fusion.5
  36.4 0.8 copy.490
  37.8 3.3 %reduce = f32[512,3,8]{2,1,0:T(4,128)S(1)} reduce(f32[512,3,1,8]{3,2,1,0:T(1,128)S(1)} %bitcast.205, f32[]{:T(128)} %broadcast.650), dimensions={2}, to_apply=%bitcast.189.reduce_sub_computation | reduce | bytes 98308
  41.1 1.3 %reshape.1284 = f32[4,1,3072]{2,1,0:T(1,128)} reshape(f32[512,3,8]{2,1,0:T(4,128)S(1)} %reduce) | data formatting | bytes 98304
  42.4 3.3 %all-to-all-start = ((f32[4,1,3072]{2,1,0:T(1,128)}), f32[4,1,3072]{2,1,0:T(1,128)S(1)}, u32[]{:S(2)}, u32[]{:S(2)}) async-start(f32[4,1,3072]{2,1,0:T(1,128)} %reshape.1284), calls=%async_computation | async-start | bytes 98304 | tf_op jit(solution)/shard_map/all_to_all | solution.py:126
  45.9 4.6 %all-to-all-done = f32[4,1,3072]{2,1,0:T(1,128)S(1)} async-done(((f32[4,1,3072]{2,1,0:T(1,128)}), f32[4,1,3072]{2,1,0:T(1,128)S(1)}, u32[]{:S(2)}, u32[]{:S(2)}) %all-to-all-start) | async-done | bytes 49184 | tf_op jit(solution)/shard_map/all_to_all | solution.py:126
  50.4 0.8 reduce.1
  51.2 1.2 %reshape.1285 = f32[512,3,1,8]{3,2,1,0:T(1,128)S(1)} reshape(f32[4,3072]{1,0:T(4,128)S(1)} %reduce.1) | data formatting | bytes 98304
  52.5 0.9 copy.491
  53.4 0.7 copy-done.6
  56.2 0.7 broadcast_multiply_fusion
  56.9 3.3 %all-to-all-start.1 = ((f32[4,8,128]{2,1,0:T(8,128)}), f32[4,8,128]{2,1,0:T(8,128)S(1)}, u32[]{:S(2)}, u32[]{:S(2)}) async-start(f32[4,8,128]{2,1,0:T(8,128)} %broadcast_multiply_fusion), calls=%async_computation.1 | async-start | bytes 32768 | tf_op jit(solution)/shard_map/all_to_all | solution.py:152
  60.2 4.6 %all-to-all-done.1 = f32[4,8,128]{2,1,0:T(8,128)S(1)} async-done(((f32[4,8,128]{2,1,0:T(8,128)}), f32[4,8,128]{2,1,0:T(8,128)S(1)}, u32[]{:S(2)}, u32[]{:S(2)}) %all-to-all-start.1) | async-done | bytes 16416 | tf_op jit(solution)/shard_map/all_to_all | solution.py:152
  64.9 3.5 %collective-permute-start.13 = (f32[3,1,2,512]{3,2,1,0:T(2,128)S(1)}, f32[3,1,2,512]{3,2,1,0:T(2,128)S(1)}, u32[]{:S(2)}, u32[]{:S(2)}) collective-permute-start(f32[3,1,2,512]{3,2,1,0:T(2,128)S(1)} %get-tuple-element.105), channel_id=1, source_target_pairs={{1,0},{2,1},{3,2},{4,3},{5,4},{6,5},{7,6},{0,7},{9,8},{10,9},{11,1... | collective-permute-start | bytes 36872 | tf_op jit(solution)/shard_map/ppermute | solution.py:26
  68.5 3.5 %collective-permute-start.21 = (f32[12,4,1,128]{3,0,2,1:T(8,128)S(1)}, f32[12,4,1,128]{3,0,2,1:T(8,128)S(1)}, u32[]{:S(2)}, u32[]{:S(2)}) collective-permute-start(f32[12,4,1,128]{3,0,2,1:T(8,128)S(1)} %get-tuple-element.65), channel_id=1, source_target_pairs={{1,0},{2,1},{3,2},{4,3},{5,4},{6,5},{7,6},{0,7},{9,8},{10,9},{11,1... | collective-permute-start | bytes 73736 | tf_op jit(solution)/shard_map/ppermute | solution.py:26
  73.0 3.5 %collective-permute-start.15 = (f32[3,1,2,512]{3,2,1,0:T(2,128)S(1)}, f32[3,1,2,512]{3,2,1,0:T(2,128)S(1)}, u32[]{:S(2)}, u32[]{:S(2)}) collective-permute-start(f32[3,1,2,512]{3,2,1,0:T(2,128)S(1)} %get-tuple-element.103), channel_id=1, source_target_pairs={{1,0},{2,1},{3,2},{4,3},{5,4},{6,5},{7,6},{0,7},{9,8},{10,9},{11,1... | collective-permute-start | bytes 36872 | tf_op jit(solution)/shard_map/ppermute | solution.py:26
  76.6 1.3 %collective-permute-done.14 = f32[3,1,2,512]{3,2,1,0:T(2,128)S(1)} collective-permute-done((f32[3,1,2,512]{3,2,1,0:T(2,128)S(1)}, f32[3,1,2,512]{3,2,1,0:T(2,128)S(1)}, u32[]{:S(2)}, u32[]{:S(2)}) %collective-permute-start.14) | collective-permute-done | bytes 12320 | tf_op jit(solution)/shard_map/ppermute | solution.py:24
  78.8 3.6 %collective-permute-start.17 = (f32[3,1,2,512]{3,2,1,0:T(2,128)S(1)}, f32[3,1,2,512]{3,2,1,0:T(2,128)S(1)}, u32[]{:S(2)}, u32[]{:S(2)}) collective-permute-start(f32[3,1,2,512]{3,2,1,0:T(2,128)S(1)} %get-tuple-element.101), channel_id=1, source_target_pairs={{1,0},{2,1},{3,2},{4,3},{5,4},{6,5},{7,6},{0,7},{9,8},{10,9},{11,1... | collective-permute-start | bytes 36872 | tf_op jit(solution)/shard_map/ppermute | solution.py:26
  82.5 1.3 %collective-permute-done.16 = f32[3,1,2,512]{3,2,1,0:T(2,128)S(1)} collective-permute-done((f32[3,1,2,512]{3,2,1,0:T(2,128)S(1)}, f32[3,1,2,512]{3,2,1,0:T(2,128)S(1)}, u32[]{:S(2)}, u32[]{:S(2)}) %collective-permute-start.16) | collective-permute-done | bytes 12320 | tf_op jit(solution)/shard_map/ppermute | solution.py:24
  84.7 3.7 %collective-permute-start.19 = (f32[3,1,2,512]{3,2,1,0:T(2,128)S(1)}, f32[3,1,2,512]{3,2,1,0:T(2,128)S(1)}, u32[]{:S(2)}, u32[]{:S(2)}) collective-permute-start(f32[3,1,2,512]{3,2,1,0:T(2,128)S(1)} %get-tuple-element.99), channel_id=1, source_target_pairs={{1,0},{2,1},{3,2},{4,3},{5,4},{6,5},{7,6},{0,7},{9,8},{10,9},{11,1... | collective-permute-start | bytes 36872 | tf_op jit(solution)/shard_map/ppermute | solution.py:26
  88.6 1.1 collective-permute-done.18
  90.3 1.4 %multiply_bitcast_fusion.2 = (f32[1,1,8,512]{3,2,1,0:T(8,128)S(1)}, f32[1,8,512]{2,1,0:T(8,128)S(1)}, f32[1,8,512]{2,1,0:T(8,128)}, f32[1,8,512]{2,1,0:T(8,128)S(1)}, f32[1,8,512]{2,1,0:T(8,128)}) fusion(f32[]{:T(128)} %bitcast.27, f32[1,8,512]{2,1,0:T(8,128)S(1)} %fusion.106, f32[1,8,512]{2,1,0:T(8,128)S(1)} %fusion.144, f32[1,8,512]{2,1,0:T(8,128)S(1)} %fusion.125, ...), kind=kLoop, calls=%fused_computation.359 | loop fusion | flops 200704 | bytes 393220 | tf_op jit(solution)/shard_map/stack | solution.py:127
  91.7 0.8 copy.509
  92.6 3.3 %reduce.2 = f32[512,3,8]{2,1,0:T(4,128)S(1)} reduce(f32[512,3,1,8]{3,2,1,0:T(1,128)S(1)} %bitcast.207, f32[]{:T(128)} %broadcast.650), dimensions={2}, to_apply=%bitcast.191.reduce_sub_computation | reduce | bytes 98308
  95.9 1.3 %reshape.1286 = f32[4,1,3072]{2,1,0:T(1,128)} reshape(f32[512,3,8]{2,1,0:T(4,128)S(1)} %reduce.2) | data formatting | bytes 98304
  97.2 3.3 %all-to-all-start.2 = ((f32[4,1,3072]{2,1,0:T(1,128)}), f32[4,1,3072]{2,1,0:T(1,128)S(1)}, u32[]{:S(2)}, u32[]{:S(2)}) async-start(f32[4,1,3072]{2,1,0:T(1,128)} %reshape.1286), calls=%async_computation.2 | async-start | bytes 98304 | tf_op jit(solution)/shard_map/all_to_all | solution.py:126
  100.6 2.0 %collective-permute-start.22 = (f32[12,4,10,1]{3,0,2,1:T(8,128)S(1)}, f32[12,4,10,1]{3,0,2,1:T(8,128)S(1)}, u32[]{:S(2)}, u32[]{:S(2)}) collective-permute-start(f32[12,4,10,1]{3,0,2,1:T(8,128)S(1)} %get-tuple-element.60), channel_id=1, source_target_pairs={{0,8},{8,16},{16,24},{24,0},{1,9},{9,17},{17,25},{25,1},{2,10},{10... | collective-permute-start | bytes 5768 | tf_op jit(solution)/shard_map/ppermute | solution.py:24
  102.6 1.0 collective-permute-start.23
  104.2 1.1 all-to-all-done.2
  105.3 0.8 reduce.3
  106.1 1.3 %reshape.1287 = f32[512,3,1,8]{3,2,1,0:T(1,128)S(1)} reshape(f32[4,3072]{1,0:T(4,128)S(1)} %reduce.3) | data formatting | bytes 98304
  107.3 0.9 copy.510
  108.3 3.3 %collective-permute-done.22 = f32[12,4,10,1]{3,0,2,1:T(8,128)S(1)} collective-permute-done((f32[12,4,10,1]{3,0,2,1:T(8,128)S(1)}, f32[12,4,10,1]{3,0,2,1:T(8,128)S(1)}, u32[]{:S(2)}, u32[]{:S(2)}) %collective-permute-start.22) | collective-permute-done | bytes 1952 | tf_op jit(solution)/shard_map/ppermute | solution.py:24
  111.6 3.6 %collective-permute-done.23 = f32[12,4,10,1]{3,0,2,1:T(8,128)S(1)} collective-permute-done((f32[12,4,10,1]{3,0,2,1:T(8,128)S(1)}, f32[12,4,10,1]{3,0,2,1:T(8,128)S(1)}, u32[]{:S(2)}, u32[]{:S(2)}) %collective-permute-start.23) | collective-permute-done | bytes 1952 | tf_op jit(solution)/shard_map/ppermute | solution.py:26
  116.0 0.7 copy.512
  (187 shorter events, 15.8 us)
Async XLA Ops:
  0.6 54.0 %copy-start = (f32[12,12]{1,0:T(8,128)S(1)}, f32[12,12]{1,0:T(8,128)}, u32[]{:S(2)}) copy-start(f32[12,12]{1,0:T(8,128)} %param.17) | copy-start | bytes 1732
  1.5 13.0 %collective-permute-start = (f32[3,1,2,512]{3,2,1,0:T(2,128)S(1)}, f32[3,1,2,512]{3,2,1,0:T(2,128)S(1)}, u32[]{:S(2)}, u32[]{:S(2)}) collective-permute-start(f32[3,1,2,512]{3,2,1,0:T(2,128)S(1)} %get-tuple-element.118), channel_id=1, source_target_pairs={{0,1},{1,2},{2,3},{3,4},{4,5},{5,6},{6,7},{7,0},{8,9},{9,10},{10,1... | collective-permute-start | bytes 36872 | tf_op jit(solution)/shard_map/ppermute | solution.py:24
  2.0 12.4 %collective-permute-start.1 = (f32[3,1,2,512]{3,2,1,0:T(2,128)S(1)}, f32[3,1,2,512]{3,2,1,0:T(2,128)S(1)}, u32[]{:S(2)}, u32[]{:S(2)}) collective-permute-start(f32[3,1,2,512]{3,2,1,0:T(2,128)S(1)} %get-tuple-element.119), channel_id=1, source_target_pairs={{1,0},{2,1},{3,2},{4,3},{5,4},{6,5},{7,6},{0,7},{9,8},{10,9},{11,1... | collective-permute-start | bytes 36872 | tf_op jit(solution)/shard_map/ppermute | solution.py:26
  7.1 3.6 %copy-start.3 = (f32[1,8,512]{2,1,0:T(8,128)S(1)}, f32[1,8,512]{2,1,0:T(8,128)}, u32[]{:S(2)}) copy-start(f32[1,8,512]{2,1,0:T(8,128)} %param.10) | copy-start | bytes 49156
  7.2 17.6 %collective-permute-start.8 = (f32[12,4,1,128]{3,0,2,1:T(8,128)S(1)}, f32[12,4,1,128]{3,0,2,1:T(8,128)S(1)}, u32[]{:S(2)}, u32[]{:S(2)}) collective-permute-start(f32[12,4,1,128]{3,0,2,1:T(8,128)S(1)} %get-tuple-element.66), channel_id=1, source_target_pairs={{0,1},{1,2},{2,3},{3,4},{4,5},{5,6},{6,7},{7,0},{8,9},{9,10},{10,1... | collective-permute-start | bytes 73736 | tf_op jit(solution)/shard_map/ppermute | solution.py:24
  7.2 17.7 %collective-permute-start.9 = (f32[12,4,1,128]{3,0,2,1:T(8,128)S(1)}, f32[12,4,1,128]{3,0,2,1:T(8,128)S(1)}, u32[]{:S(2)}, u32[]{:S(2)}) collective-permute-start(f32[12,4,1,128]{3,0,2,1:T(8,128)S(1)} %get-tuple-element.67), channel_id=1, source_target_pairs={{1,0},{2,1},{3,2},{4,3},{5,4},{6,5},{7,6},{0,7},{9,8},{10,9},{11,1... | collective-permute-start | bytes 73736 | tf_op jit(solution)/shard_map/ppermute | solution.py:26
  10.8 0.7 copy-start.4
  11.6 0.7 copy-start.1
  12.4 0.7 copy-start.8
  13.1 1.4 %copy-start.7 = (f32[1,8,512]{2,1,0:T(8,128)S(1)}, f32[1,8,512]{2,1,0:T(8,128)}, u32[]{:S(2)}) copy-start(f32[1,8,512]{2,1,0:T(8,128)} %param.12) | copy-start | bytes 49156
  13.1 0.7 copy-start.11
  15.3 5.0 %collective-permute-start.2 = (f32[3,1,2,512]{3,2,1,0:T(2,128)S(1)}, f32[3,1,2,512]{3,2,1,0:T(2,128)S(1)}, u32[]{:S(2)}, u32[]{:S(2)}) collective-permute-start(f32[3,1,2,512]{3,2,1,0:T(2,128)S(1)} %get-tuple-element.116), channel_id=1, source_target_pairs={{0,1},{1,2},{2,3},{3,4},{4,5},{5,6},{6,7},{7,0},{8,9},{9,10},{10,1... | collective-permute-start | bytes 36872 | tf_op jit(solution)/shard_map/ppermute | solution.py:24
  15.4 4.9 %collective-permute-start.3 = (f32[3,1,2,512]{3,2,1,0:T(2,128)S(1)}, f32[3,1,2,512]{3,2,1,0:T(2,128)S(1)}, u32[]{:S(2)}, u32[]{:S(2)}) collective-permute-start(f32[3,1,2,512]{3,2,1,0:T(2,128)S(1)} %get-tuple-element.117), channel_id=1, source_target_pairs={{1,0},{2,1},{3,2},{4,3},{5,4},{6,5},{7,6},{0,7},{9,8},{10,9},{11,1... | collective-permute-start | bytes 36872 | tf_op jit(solution)/shard_map/ppermute | solution.py:26
  21.0 3.8 %copy-start.2 = (f32[12,4,8,128]{3,2,1,0:T(8,128)S(1)}, f32[12,4,8,128]{3,2,1,0:T(8,128)}, u32[]{:S(2)}) copy-start(f32[12,4,8,128]{3,2,1,0:T(8,128)} %param.16) | copy-start | bytes 589828
  21.2 8.3 %collective-permute-start.4 = (f32[3,1,2,512]{3,2,1,0:T(2,128)S(1)}, f32[3,1,2,512]{3,2,1,0:T(2,128)S(1)}, u32[]{:S(2)}, u32[]{:S(2)}) collective-permute-start(f32[3,1,2,512]{3,2,1,0:T(2,128)S(1)} %get-tuple-element.114), channel_id=1, source_target_pairs={{0,1},{1,2},{2,3},{3,4},{4,5},{5,6},{6,7},{7,0},{8,9},{9,10},{10,1... | collective-permute-start | bytes 36872 | tf_op jit(solution)/shard_map/ppermute | solution.py:24
  21.2 8.2 %collective-permute-start.5 = (f32[3,1,2,512]{3,2,1,0:T(2,128)S(1)}, f32[3,1,2,512]{3,2,1,0:T(2,128)S(1)}, u32[]{:S(2)}, u32[]{:S(2)}) collective-permute-start(f32[3,1,2,512]{3,2,1,0:T(2,128)S(1)} %get-tuple-element.115), channel_id=1, source_target_pairs={{1,0},{2,1},{3,2},{4,3},{5,4},{6,5},{7,6},{0,7},{9,8},{10,9},{11,1... | collective-permute-start | bytes 36872 | tf_op jit(solution)/shard_map/ppermute | solution.py:26
  24.9 0.6 copy-start.5
  26.5 26.9 %collective-permute-start.10 = (f32[12,4,10,1]{3,0,2,1:T(8,128)}, f32[12,4,10,1]{3,0,2,1:T(8,128)S(1)}, u32[]{:S(2)}, u32[]{:S(2)}) collective-permute-start(f32[12,4,10,1]{3,0,2,1:T(8,128)} %get-tuple-element.62), channel_id=1, source_target_pairs={{0,8},{8,16},{16,24},{24,0},{1,9},{9,17},{17,25},{25,1},{2,10},{10... | collective-permute-start | bytes 5768 | tf_op jit(solution)/shard_map/ppermute | solution.py:24
  28.5 25.0 %collective-permute-start.11 = (f32[12,4,10,1]{3,0,2,1:T(8,128)S(1)}, f32[12,4,10,1]{3,0,2,1:T(8,128)S(1)}, u32[]{:S(2)}, u32[]{:S(2)}) collective-permute-start(f32[12,4,10,1]{3,0,2,1:T(8,128)S(1)} %get-tuple-element.63), channel_id=1, source_target_pairs={{8,0},{16,8},{24,16},{0,24},{9,1},{17,9},{25,17},{1,25},{10,2},{18... | collective-permute-start | bytes 5768 | tf_op jit(solution)/shard_map/ppermute | solution.py:26
  30.2 5.0 %collective-permute-start.6 = (f32[3,1,2,512]{3,2,1,0:T(2,128)S(1)}, f32[3,1,2,512]{3,2,1,0:T(2,128)S(1)}, u32[]{:S(2)}, u32[]{:S(2)}) collective-permute-start(f32[3,1,2,512]{3,2,1,0:T(2,128)S(1)} %get-tuple-element.112), channel_id=1, source_target_pairs={{0,1},{1,2},{2,3},{3,4},{4,5},{5,6},{6,7},{7,0},{8,9},{9,10},{10,1... | collective-permute-start | bytes 36872 | tf_op jit(solution)/shard_map/ppermute | solution.py:24
  30.2 4.9 %collective-permute-start.7 = (f32[3,1,2,512]{3,2,1,0:T(2,128)S(1)}, f32[3,1,2,512]{3,2,1,0:T(2,128)S(1)}, u32[]{:S(2)}, u32[]{:S(2)}) collective-permute-start(f32[3,1,2,512]{3,2,1,0:T(2,128)S(1)} %get-tuple-element.113), channel_id=1, source_target_pairs={{1,0},{2,1},{3,2},{4,3},{5,4},{6,5},{7,6},{0,7},{9,8},{10,9},{11,1... | collective-permute-start | bytes 36872 | tf_op jit(solution)/shard_map/ppermute | solution.py:26
  42.4 8.1 %all-to-all-start = ((f32[4,1,3072]{2,1,0:T(1,128)}), f32[4,1,3072]{2,1,0:T(1,128)S(1)}, u32[]{:S(2)}, u32[]{:S(2)}) async-start(f32[4,1,3072]{2,1,0:T(1,128)} %reshape.1284), calls=%async_computation | async-start | bytes 98304 | tf_op jit(solution)/shard_map/all_to_all | solution.py:126
  53.4 0.8 copy-start.6
  54.6 0.7 copy-start.9
  55.6 0.7 copy-start.10
  56.9 7.9 %all-to-all-start.1 = ((f32[4,8,128]{2,1,0:T(8,128)}), f32[4,8,128]{2,1,0:T(8,128)S(1)}, u32[]{:S(2)}, u32[]{:S(2)}) async-start(f32[4,8,128]{2,1,0:T(8,128)} %broadcast_multiply_fusion), calls=%async_computation.1 | async-start | bytes 32768 | tf_op jit(solution)/shard_map/all_to_all | solution.py:152
  64.8 7.2 %collective-permute-start.12 = (f32[3,1,2,512]{3,2,1,0:T(2,128)S(1)}, f32[3,1,2,512]{3,2,1,0:T(2,128)S(1)}, u32[]{:S(2)}, u32[]{:S(2)}) collective-permute-start(f32[3,1,2,512]{3,2,1,0:T(2,128)S(1)} %get-tuple-element.104), channel_id=1, source_target_pairs={{0,1},{1,2},{2,3},{3,4},{4,5},{5,6},{6,7},{7,0},{8,9},{9,10},{10,1... | collective-permute-start | bytes 36872 | tf_op jit(solution)/shard_map/ppermute | solution.py:24
  64.9 7.1 %collective-permute-start.13 = (f32[3,1,2,512]{3,2,1,0:T(2,128)S(1)}, f32[3,1,2,512]{3,2,1,0:T(2,128)S(1)}, u32[]{:S(2)}, u32[]{:S(2)}) collective-permute-start(f32[3,1,2,512]{3,2,1,0:T(2,128)S(1)} %get-tuple-element.105), channel_id=1, source_target_pairs={{1,0},{2,1},{3,2},{4,3},{5,4},{6,5},{7,6},{0,7},{9,8},{10,9},{11,1... | collective-permute-start | bytes 36872 | tf_op jit(solution)/shard_map/ppermute | solution.py:26
  68.5 8.1 %collective-permute-start.20 = (f32[12,4,1,128]{3,0,2,1:T(8,128)S(1)}, f32[12,4,1,128]{3,0,2,1:T(8,128)S(1)}, u32[]{:S(2)}, u32[]{:S(2)}) collective-permute-start(f32[12,4,1,128]{3,0,2,1:T(8,128)S(1)} %get-tuple-element.64), channel_id=1, source_target_pairs={{0,1},{1,2},{2,3},{3,4},{4,5},{5,6},{6,7},{7,0},{8,9},{9,10},{10,1... | collective-permute-start | bytes 73736 | tf_op jit(solution)/shard_map/ppermute | solution.py:24
  68.5 8.1 %collective-permute-start.21 = (f32[12,4,1,128]{3,0,2,1:T(8,128)S(1)}, f32[12,4,1,128]{3,0,2,1:T(8,128)S(1)}, u32[]{:S(2)}, u32[]{:S(2)}) collective-permute-start(f32[12,4,1,128]{3,0,2,1:T(8,128)S(1)} %get-tuple-element.65), channel_id=1, source_target_pairs={{1,0},{2,1},{3,2},{4,3},{5,4},{6,5},{7,6},{0,7},{9,8},{10,9},{11,1... | collective-permute-start | bytes 73736 | tf_op jit(solution)/shard_map/ppermute | solution.py:26
  72.9 5.0 %collective-permute-start.14 = (f32[3,1,2,512]{3,2,1,0:T(2,128)S(1)}, f32[3,1,2,512]{3,2,1,0:T(2,128)S(1)}, u32[]{:S(2)}, u32[]{:S(2)}) collective-permute-start(f32[3,1,2,512]{3,2,1,0:T(2,128)S(1)} %get-tuple-element.102), channel_id=1, source_target_pairs={{0,1},{1,2},{2,3},{3,4},{4,5},{5,6},{6,7},{7,0},{8,9},{9,10},{10,1... | collective-permute-start | bytes 36872 | tf_op jit(solution)/shard_map/ppermute | solution.py:24
  73.0 4.9 %collective-permute-start.15 = (f32[3,1,2,512]{3,2,1,0:T(2,128)S(1)}, f32[3,1,2,512]{3,2,1,0:T(2,128)S(1)}, u32[]{:S(2)}, u32[]{:S(2)}) collective-permute-start(f32[3,1,2,512]{3,2,1,0:T(2,128)S(1)} %get-tuple-element.103), channel_id=1, source_target_pairs={{1,0},{2,1},{3,2},{4,3},{5,4},{6,5},{7,6},{0,7},{9,8},{10,9},{11,1... | collective-permute-start | bytes 36872 | tf_op jit(solution)/shard_map/ppermute | solution.py:26
  78.8 5.0 %collective-permute-start.16 = (f32[3,1,2,512]{3,2,1,0:T(2,128)S(1)}, f32[3,1,2,512]{3,2,1,0:T(2,128)S(1)}, u32[]{:S(2)}, u32[]{:S(2)}) collective-permute-start(f32[3,1,2,512]{3,2,1,0:T(2,128)S(1)} %get-tuple-element.100), channel_id=1, source_target_pairs={{0,1},{1,2},{2,3},{3,4},{4,5},{5,6},{6,7},{7,0},{8,9},{9,10},{10,1... | collective-permute-start | bytes 36872 | tf_op jit(solution)/shard_map/ppermute | solution.py:24
  78.8 5.0 %collective-permute-start.17 = (f32[3,1,2,512]{3,2,1,0:T(2,128)S(1)}, f32[3,1,2,512]{3,2,1,0:T(2,128)S(1)}, u32[]{:S(2)}, u32[]{:S(2)}) collective-permute-start(f32[3,1,2,512]{3,2,1,0:T(2,128)S(1)} %get-tuple-element.101), channel_id=1, source_target_pairs={{1,0},{2,1},{3,2},{4,3},{5,4},{6,5},{7,6},{0,7},{9,8},{10,9},{11,1... | collective-permute-start | bytes 36872 | tf_op jit(solution)/shard_map/ppermute | solution.py:26
  84.7 5.0 %collective-permute-start.18 = (f32[3,1,2,512]{3,2,1,0:T(2,128)S(1)}, f32[3,1,2,512]{3,2,1,0:T(2,128)S(1)}, u32[]{:S(2)}, u32[]{:S(2)}) collective-permute-start(f32[3,1,2,512]{3,2,1,0:T(2,128)S(1)} %get-tuple-element.98), channel_id=1, source_target_pairs={{0,1},{1,2},{2,3},{3,4},{4,5},{5,6},{6,7},{7,0},{8,9},{9,10},{10,1... | collective-permute-start | bytes 36872 | tf_op jit(solution)/shard_map/ppermute | solution.py:24
  84.7 5.2 %collective-permute-start.19 = (f32[3,1,2,512]{3,2,1,0:T(2,128)S(1)}, f32[3,1,2,512]{3,2,1,0:T(2,128)S(1)}, u32[]{:S(2)}, u32[]{:S(2)}) collective-permute-start(f32[3,1,2,512]{3,2,1,0:T(2,128)S(1)} %get-tuple-element.99), channel_id=1, source_target_pairs={{1,0},{2,1},{3,2},{4,3},{5,4},{6,5},{7,6},{0,7},{9,8},{10,9},{11,1... | collective-permute-start | bytes 36872 | tf_op jit(solution)/shard_map/ppermute | solution.py:26
  97.2 8.2 %all-to-all-start.2 = ((f32[4,1,3072]{2,1,0:T(1,128)}), f32[4,1,3072]{2,1,0:T(1,128)S(1)}, u32[]{:S(2)}, u32[]{:S(2)}) async-start(f32[4,1,3072]{2,1,0:T(1,128)} %reshape.1286), calls=%async_computation.2 | async-start | bytes 98304 | tf_op jit(solution)/shard_map/all_to_all | solution.py:126
  100.6 11.0 %collective-permute-start.22 = (f32[12,4,10,1]{3,0,2,1:T(8,128)S(1)}, f32[12,4,10,1]{3,0,2,1:T(8,128)S(1)}, u32[]{:S(2)}, u32[]{:S(2)}) collective-permute-start(f32[12,4,10,1]{3,0,2,1:T(8,128)S(1)} %get-tuple-element.60), channel_id=1, source_target_pairs={{0,8},{8,16},{16,24},{24,0},{1,9},{9,17},{17,25},{25,1},{2,10},{10... | collective-permute-start | bytes 5768 | tf_op jit(solution)/shard_map/ppermute | solution.py:24
  102.6 12.5 %collective-permute-start.23 = (f32[12,4,10,1]{3,0,2,1:T(8,128)S(1)}, f32[12,4,10,1]{3,0,2,1:T(8,128)S(1)}, u32[]{:S(2)}, u32[]{:S(2)}) collective-permute-start(f32[12,4,10,1]{3,0,2,1:T(8,128)S(1)} %get-tuple-element.61), channel_id=1, source_target_pairs={{8,0},{16,8},{24,16},{0,24},{9,1},{17,9},{25,17},{1,25},{10,2},{18... | collective-permute-start | bytes 5768 | tf_op jit(solution)/shard_map/ppermute | solution.py:26
where the time goes:
time: 118 us; the launch traced here: 117 us
  starting transfers between devices  52.9 us (45%)
  waiting for transfers between devices  23.8 us (20%)
  local copies, waits for them, and re-layouts  22.7 us (19%)
  other arithmetic  14.9 us (13%)
  between operations  1.32 us (1%)
    ppermute x12, starting transfers between devices, padded_2(): lax.ppermute(head, axis, [((i + 1) % count, i) for i in range(count)])  38.1 us
    unnamed x33, local copies, waits for them, and re-layouts  12.3 us
    ppermute x12, waiting for transfers between devices, padded_2(): lax.ppermute(tail, axis, [(i, (i + 1) % count) for i in range(count)])  9.59 us
    unnamed x2, other arithmetic  6.67 us
    all_to_all x2, starting transfers between devices, body(): lax.all_to_all(jnp.stack([zonal_mean, merid_mean, kappa_rows]), 'sect', s...  6.55 us
    all_to_all x2, waiting for transfers between devices, body(): lax.all_to_all(jnp.stack([zonal_mean, merid_mean, kappa_rows]), 'sect', s...  5.67 us
    ppermute x12, starting transfers between devices, padded_2(): lax.ppermute(tail, axis, [(i, (i + 1) % count) for i in range(count)])  4.97 us
    all_to_all x1, waiting for transfers between devices, body(): lax.all_to_all(heat_cols, 'sect', split_axis=0, concat_axis=2, tiled=True)  4.61 us
  transfers between devices with their start and end apart: 27, of which 12 were waited for; matrix products, arithmetic and copies ran while one was open for 18% of the time, Pallas kernels for 0%

commit v1 on v0

--- a/solution.py
+++ b/solution.py
@@ -12,6 +12,22 @@
 heat_coupling = 0.05
 tracer_step = 0.5
 stir_gain = 4.0
+
+
+def pairwise_exchange(x, axis, split, join):
+    ways, here = (lax.axis_size(axis), lax.axis_index(axis))
+    width = x.shape[split] // ways
+    shape = list(x.shape)
+    shape[split] = width
+    height = shape[join]
+    shape[join] = height * ways
+    full = jnp.zeros(shape, x.dtype)
+    for mask in range(ways):
+        part = lax.dynamic_slice_in_dim(x, (here ^ mask) * width, width, axis=split)
+        if mask:
+            part = lax.ppermute(part, axis, [(d, d ^ mask) for d in range(ways)])
+        full = lax.dynamic_update_slice_in_dim(full, part, (here ^ mask) * height, axis=join)
+    return full
 
 
 def padded_2(cells, sides, width):
@@ -149,7 +165,7 @@
             heat_cols = light[:, None, None] * jnp.einsum(
                 "k,kzyx->zyx", absorb, conc, precision=lax.Precision.HIGHEST
             )
-            forcing = lax.all_to_all(heat_cols, "sect", split_axis=0, concat_axis=2, tiled=True)
+            forcing = pairwise_exchange(heat_cols, "sect", 0, 2)
     return (conc, zonal, merid, height)
 
 

time: 118 us -> 115 us (0.975)
  waiting for transfers between devices: 23.8 us -> 21.1 us
    all_to_all x1 -> x0, waiting for transfers between devices: 4.61 us -> none  [body(): lax.all_to_all(heat_cols, 'sect', split_axis=0, concat_axis=2, tiled=True)]
    ppermute x0 -> x3, starting transfers between devices: none -> 3.55 us  [pairwise_exchange(): part = lax.ppermute(part, axis, [(d, d ^ mask) for d in range(ways)])]
    all_to_all x1 -> x0, starting transfers between devices: 3.25 us -> none  [body(): lax.all_to_all(heat_cols, 'sect', split_axis=0, concat_axis=2, tiled=True)]
    ppermute x0 -> x3, waiting for transfers between devices: none -> 2.14 us  [pairwise_exchange(): part = lax.ppermute(part, axis, [(d, d ^ mask) for d in range(ways)])]
  transfers between devices with their start and end apart: 27 -> 29, of which waited for: 12 -> 13; matrix products, arithmetic and copies ran while one was open for 18% -> 18% of each run, Pallas kernels for 0% -> 0%
where the time goes in v1:
time: 115 us; the launch traced here: 114 us
  starting transfers between devices  53.6 us (47%)
  local copies, waits for them, and re-layouts  22.6 us (20%)
  waiting for transfers between devices  21.1 us (18%)
  other arithmetic  14.2 us (12%)
  between operations  1.35 us (1%)
    ppermute x12, starting transfers between devices, padded_2(): lax.ppermute(head, axis, [((i + 1) % count, i) for i in range(count)])  38.1 us
    unnamed x33, local copies, waits for them, and re-layouts  12.3 us
    ppermute x12, waiting for transfers between devices, padded_2(): lax.ppermute(tail, axis, [(i, (i + 1) % count) for i in range(count)])  9.31 us
    all_to_all x2, starting transfers between devices, body(): lax.all_to_all(jnp.stack([zonal_mean, merid_mean, kappa_rows]), 'sect', s...  6.9 us
    unnamed x2, other arithmetic  6.67 us
    all_to_all x2, waiting for transfers between devices, body(): lax.all_to_all(jnp.stack([zonal_mean, merid_mean, kappa_rows]), 'sect', s...  5.67 us
    ppermute x12, starting transfers between devices, padded_2(): lax.ppermute(tail, axis, [(i, (i + 1) % count) for i in range(count)])  5.01 us
    ppermute x12, waiting for transfers between devices, padded_2(): lax.ppermute(head, axis, [((i + 1) % count, i) for i in range(count)])  3.96 us
  transfers between devices with their start and end apart: 29, of which 13 were waited for; matrix products, arithmetic and copies ran while one was open for 18% of the time, Pallas kernels for 0%

profile of v1, /device:TPU:0, one launch (start us, length us, event | category | flops | bytes accessed | tf_op | source)
XLA Modules:
  0.0 113.9 jit_solution(9125977224039735840)
XLA Ops:
  0.6 0.8 pad_maximum_fusion.46
  2.0 4.1 %collective-permute-start.1 = (f32[3,1,2,512]{3,2,1,0:T(2,128)S(1)}, f32[3,1,2,512]{3,2,1,0:T(2,128)S(1)}, u32[]{:S(2)}, u32[]{:S(2)}) collective-permute-start(f32[3,1,2,512]{3,2,1,0:T(2,128)S(1)} %get-tuple-element.119), channel_id=1, source_target_pairs={{1,0},{2,1},{3,2},{4,3},{5,4},{6,5},{7,6},{0,7},{9,8},{10,9},{11,1... | collective-permute-start | bytes 36872 | tf_op jit(solution)/shard_map/ppermute | solution.py:42
  6.1 1.0 copy.455
  7.2 3.5 %collective-permute-start.9 = (f32[12,4,1,128]{3,0,2,1:T(8,128)S(1)}, f32[12,4,1,128]{3,0,2,1:T(8,128)S(1)}, u32[]{:S(2)}, u32[]{:S(2)}) collective-permute-start(f32[12,4,1,128]{3,0,2,1:T(8,128)S(1)} %get-tuple-element.67), channel_id=1, source_target_pairs={{1,0},{2,1},{3,2},{4,3},{5,4},{6,5},{7,6},{0,7},{9,8},{10,9},{11,1... | collective-permute-start | bytes 73736 | tf_op jit(solution)/shard_map/ppermute | solution.py:42
  12.4 0.7 copy-done.8
  15.3 3.5 %collective-permute-start.3 = (f32[3,1,2,512]{3,2,1,0:T(2,128)S(1)}, f32[3,1,2,512]{3,2,1,0:T(2,128)S(1)}, u32[]{:S(2)}, u32[]{:S(2)}) collective-permute-start(f32[3,1,2,512]{3,2,1,0:T(2,128)S(1)} %get-tuple-element.117), channel_id=1, source_target_pairs={{1,0},{2,1},{3,2},{4,3},{5,4},{6,5},{7,6},{0,7},{9,8},{10,9},{11,1... | collective-permute-start | bytes 36872 | tf_op jit(solution)/shard_map/ppermute | solution.py:42
  18.9 1.3 %collective-permute-done.2 = f32[3,1,2,512]{3,2,1,0:T(2,128)S(1)} collective-permute-done((f32[3,1,2,512]{3,2,1,0:T(2,128)S(1)}, f32[3,1,2,512]{3,2,1,0:T(2,128)S(1)}, u32[]{:S(2)}, u32[]{:S(2)}) %collective-permute-start.2) | collective-permute-done | bytes 12320 | tf_op jit(solution)/shard_map/ppermute | solution.py:40
  21.2 3.6 %collective-permute-start.5 = (f32[3,1,2,512]{3,2,1,0:T(2,128)S(1)}, f32[3,1,2,512]{3,2,1,0:T(2,128)S(1)}, u32[]{:S(2)}, u32[]{:S(2)}) collective-permute-start(f32[3,1,2,512]{3,2,1,0:T(2,128)S(1)} %get-tuple-element.115), channel_id=1, source_target_pairs={{1,0},{2,1},{3,2},{4,3},{5,4},{6,5},{7,6},{0,7},{9,8},{10,9},{11,1... | collective-permute-start | bytes 36872 | tf_op jit(solution)/shard_map/ppermute | solution.py:42
  25.5 0.9 fusion.259
  26.4 1.9 %collective-permute-start.10 = (f32[12,4,10,1]{3,0,2,1:T(8,128)}, f32[12,4,10,1]{3,0,2,1:T(8,128)S(1)}, u32[]{:S(2)}, u32[]{:S(2)}) collective-permute-start(f32[12,4,10,1]{3,0,2,1:T(8,128)} %get-tuple-element.62), channel_id=1, source_target_pairs={{0,8},{8,16},{16,24},{24,0},{1,9},{9,17},{17,25},{25,1},{2,10},{10... | collective-permute-start | bytes 5768 | tf_op jit(solution)/shard_map/ppermute | solution.py:40
  28.4 1.0 collective-permute-start.11
  30.1 3.5 %collective-permute-start.7 = (f32[3,1,2,512]{3,2,1,0:T(2,128)S(1)}, f32[3,1,2,512]{3,2,1,0:T(2,128)S(1)}, u32[]{:S(2)}, u32[]{:S(2)}) collective-permute-start(f32[3,1,2,512]{3,2,1,0:T(2,128)S(1)} %get-tuple-element.113), channel_id=1, source_target_pairs={{1,0},{2,1},{3,2},{4,3},{5,4},{6,5},{7,6},{0,7},{9,8},{10,9},{11,1... | collective-permute-start | bytes 36872 | tf_op jit(solution)/shard_map/ppermute | solution.py:42
  33.8 1.3 %collective-permute-done.6 = f32[3,1,2,512]{3,2,1,0:T(2,128)S(1)} collective-permute-done((f32[3,1,2,512]{3,2,1,0:T(2,128)S(1)}, f32[3,1,2,512]{3,2,1,0:T(2,128)S(1)}, u32[]{:S(2)}, u32[]{:S(2)}) %collective-permute-start.6) | collective-permute-done | bytes 12320 | tf_op jit(solution)/shard_map/ppermute | solution.py:40
  35.5 0.7 multiply_bitcast_fusion.5
  36.3 0.8 copy.442
  37.7 3.3 %reduce = f32[512,3,8]{2,1,0:T(4,128)S(1)} reduce(f32[512,3,1,8]{3,2,1,0:T(1,128)S(1)} %bitcast.196, f32[]{:T(128)} %broadcast.636), dimensions={2}, to_apply=%bitcast.180.reduce_sub_computation | reduce | bytes 98308
  41.0 1.3 %reshape.1268 = f32[4,1,3072]{2,1,0:T(1,128)} reshape(f32[512,3,8]{2,1,0:T(4,128)S(1)} %reduce) | data formatting | bytes 98304
  42.3 3.3 %all-to-all-start = ((f32[4,1,3072]{2,1,0:T(1,128)}), f32[4,1,3072]{2,1,0:T(1,128)S(1)}, u32[]{:S(2)}, u32[]{:S(2)}) async-start(f32[4,1,3072]{2,1,0:T(1,128)} %reshape.1268), calls=%async_computation | async-start | bytes 98304 | tf_op jit(solution)/shard_map/all_to_all | solution.py:142
  45.8 4.6 %all-to-all-done = f32[4,1,3072]{2,1,0:T(1,128)S(1)} async-done(((f32[4,1,3072]{2,1,0:T(1,128)}), f32[4,1,3072]{2,1,0:T(1,128)S(1)}, u32[]{:S(2)}, u32[]{:S(2)}) %all-to-all-start) | async-done | bytes 49184 | tf_op jit(solution)/shard_map/all_to_all | solution.py:142
  50.3 0.8 reduce.1
  51.1 1.2 %reshape.1269 = f32[512,3,1,8]{3,2,1,0:T(1,128)S(1)} reshape(f32[4,3072]{1,0:T(4,128)S(1)} %reduce.1) | data formatting | bytes 98304
  52.3 0.9 copy.443
  56.2 0.8 collective-permute-start.12
  57.4 2.4 %collective-permute-start.14 = (f32[1,8,128]{2,1,0:T(8,128)S(1)}, f32[1,8,128]{2,1,0:T(8,128)S(1)}, u32[]{:S(2)}, u32[]{:S(2)}) collective-permute-start(f32[1,8,128]{2,1,0:T(8,128)S(1)} %get-tuple-element.228), channel_id=1, source_target_pairs={{0,24},{8,16},{16,8},{24,0},{1,25},{9,17},{17,9},{25,1},{2,26},{10... | collective-permute-start | bytes 12296 | tf_op jit(solution)/shard_map/ppermute | solution.py:28
  59.8 0.8 collective-permute-done.13
  60.6 1.3 %collective-permute-done.14 = f32[1,8,128]{2,1,0:T(8,128)S(1)} collective-permute-done((f32[1,8,128]{2,1,0:T(8,128)S(1)}, f32[1,8,128]{2,1,0:T(8,128)S(1)}, u32[]{:S(2)}, u32[]{:S(2)}) %collective-permute-start.14) | collective-permute-done | bytes 4128 | tf_op jit(solution)/shard_map/ppermute | solution.py:28
  62.0 3.5 %collective-permute-start.16 = (f32[3,1,2,512]{3,2,1,0:T(2,128)S(1)}, f32[3,1,2,512]{3,2,1,0:T(2,128)S(1)}, u32[]{:S(2)}, u32[]{:S(2)}) collective-permute-start(f32[3,1,2,512]{3,2,1,0:T(2,128)S(1)} %get-tuple-element.105), channel_id=1, source_target_pairs={{1,0},{2,1},{3,2},{4,3},{5,4},{6,5},{7,6},{0,7},{9,8},{10,9},{11,1... | collective-permute-start | bytes 36872 | tf_op jit(solution)/shard_map/ppermute | solution.py:42
  65.6 3.5 %collective-permute-start.24 = (f32[12,4,1,128]{3,0,2,1:T(8,128)S(1)}, f32[12,4,1,128]{3,0,2,1:T(8,128)S(1)}, u32[]{:S(2)}, u32[]{:S(2)}) collective-permute-start(f32[12,4,1,128]{3,0,2,1:T(8,128)S(1)} %get-tuple-element.65), channel_id=1, source_target_pairs={{1,0},{2,1},{3,2},{4,3},{5,4},{6,5},{7,6},{0,7},{9,8},{10,9},{11,1... | collective-permute-start | bytes 73736 | tf_op jit(solution)/shard_map/ppermute | solution.py:42
  70.1 3.5 %collective-permute-start.18 = (f32[3,1,2,512]{3,2,1,0:T(2,128)S(1)}, f32[3,1,2,512]{3,2,1,0:T(2,128)S(1)}, u32[]{:S(2)}, u32[]{:S(2)}) collective-permute-start(f32[3,1,2,512]{3,2,1,0:T(2,128)S(1)} %get-tuple-element.103), channel_id=1, source_target_pairs={{1,0},{2,1},{3,2},{4,3},{5,4},{6,5},{7,6},{0,7},{9,8},{10,9},{11,1... | collective-permute-start | bytes 36872 | tf_op jit(solution)/shard_map/ppermute | solution.py:42
  73.7 1.3 %collective-permute-done.17 = f32[3,1,2,512]{3,2,1,0:T(2,128)S(1)} collective-permute-done((f32[3,1,2,512]{3,2,1,0:T(2,128)S(1)}, f32[3,1,2,512]{3,2,1,0:T(2,128)S(1)}, u32[]{:S(2)}, u32[]{:S(2)}) %collective-permute-start.17) | collective-permute-done | bytes 12320 | tf_op jit(solution)/shard_map/ppermute | solution.py:40
  76.0 3.6 %collective-permute-start.20 = (f32[3,1,2,512]{3,2,1,0:T(2,128)S(1)}, f32[3,1,2,512]{3,2,1,0:T(2,128)S(1)}, u32[]{:S(2)}, u32[]{:S(2)}) collective-permute-start(f32[3,1,2,512]{3,2,1,0:T(2,128)S(1)} %get-tuple-element.101), channel_id=1, source_target_pairs={{1,0},{2,1},{3,2},{4,3},{5,4},{6,5},{7,6},{0,7},{9,8},{10,9},{11,1... | collective-permute-start | bytes 36872 | tf_op jit(solution)/shard_map/ppermute | solution.py:42
  79.6 1.3 %collective-permute-done.19 = f32[3,1,2,512]{3,2,1,0:T(2,128)S(1)} collective-permute-done((f32[3,1,2,512]{3,2,1,0:T(2,128)S(1)}, f32[3,1,2,512]{3,2,1,0:T(2,128)S(1)}, u32[]{:S(2)}, u32[]{:S(2)}) %collective-permute-start.19) | collective-permute-done | bytes 12320 | tf_op jit(solution)/shard_map/ppermute | solution.py:40
  81.9 3.7 %collective-permute-start.22 = (f32[3,1,2,512]{3,2,1,0:T(2,128)S(1)}, f32[3,1,2,512]{3,2,1,0:T(2,128)S(1)}, u32[]{:S(2)}, u32[]{:S(2)}) collective-permute-start(f32[3,1,2,512]{3,2,1,0:T(2,128)S(1)} %get-tuple-element.99), channel_id=1, source_target_pairs={{1,0},{2,1},{3,2},{4,3},{5,4},{6,5},{7,6},{0,7},{9,8},{10,9},{11,1... | collective-permute-start | bytes 36872 | tf_op jit(solution)/shard_map/ppermute | solution.py:42
  85.7 1.1 collective-permute-done.21
  87.4 1.3 %multiply_bitcast_fusion.2 = (f32[1,1,8,512]{3,2,1,0:T(8,128)S(1)}, f32[1,8,512]{2,1,0:T(8,128)S(1)}, f32[1,8,512]{2,1,0:T(8,128)}, f32[1,8,512]{2,1,0:T(8,128)S(1)}, f32[1,8,512]{2,1,0:T(8,128)}) fusion(f32[]{:T(128)} %bitcast.27, f32[1,8,512]{2,1,0:T(8,128)S(1)} %fusion.106, f32[1,8,512]{2,1,0:T(8,128)S(1)} %fusion.144, f32[1,8,512]{2,1,0:T(8,128)S(1)} %fusion.125, ...), kind=kLoop, calls=%fused_computation.359 | loop fusion | flops 200704 | bytes 393220 | tf_op jit(solution)/shard_map/stack | solution.py:143
  88.8 0.8 copy.461
  89.6 3.3 %reduce.2 = f32[512,3,8]{2,1,0:T(4,128)S(1)} reduce(f32[512,3,1,8]{3,2,1,0:T(1,128)S(1)} %bitcast.198, f32[]{:T(128)} %broadcast.636), dimensions={2}, to_apply=%bitcast.182.reduce_sub_computation | reduce | bytes 98308
  93.0 1.3 %reshape.1270 = f32[4,1,3072]{2,1,0:T(1,128)} reshape(f32[512,3,8]{2,1,0:T(4,128)S(1)} %reduce.2) | data formatting | bytes 98304
  94.2 3.6 %all-to-all-start.1 = ((f32[4,1,3072]{2,1,0:T(1,128)}), f32[4,1,3072]{2,1,0:T(1,128)S(1)}, u32[]{:S(2)}, u32[]{:S(2)}) async-start(f32[4,1,3072]{2,1,0:T(1,128)} %reshape.1270), calls=%async_computation.1 | async-start | bytes 98304 | tf_op jit(solution)/shard_map/all_to_all | solution.py:142
  98.0 2.1 %collective-permute-start.25 = (f32[12,4,10,1]{3,0,2,1:T(8,128)S(1)}, f32[12,4,10,1]{3,0,2,1:T(8,128)S(1)}, u32[]{:S(2)}, u32[]{:S(2)}) collective-permute-start(f32[12,4,10,1]{3,0,2,1:T(8,128)S(1)} %get-tuple-element.60), channel_id=1, source_target_pairs={{0,8},{8,16},{16,24},{24,0},{1,9},{9,17},{17,25},{25,1},{2,10},{10... | collective-permute-start | bytes 5768 | tf_op jit(solution)/shard_map/ppermute | solution.py:40
  100.1 1.0 collective-permute-start.26
  101.7 1.1 all-to-all-done.1
  102.8 0.8 reduce.3
  103.5 1.2 %reshape.1271 = f32[512,3,1,8]{3,2,1,0:T(1,128)S(1)} reshape(f32[4,3072]{1,0:T(4,128)S(1)} %reduce.3) | data formatting | bytes 98304
  104.8 0.9 copy.462
  105.8 3.0 %collective-permute-done.25 = f32[12,4,10,1]{3,0,2,1:T(8,128)S(1)} collective-permute-done((f32[12,4,10,1]{3,0,2,1:T(8,128)S(1)}, f32[12,4,10,1]{3,0,2,1:T(8,128)S(1)}, u32[]{:S(2)}, u32[]{:S(2)}) %collective-permute-start.25) | collective-permute-done | bytes 1952 | tf_op jit(solution)/shard_map/ppermute | solution.py:40
  108.8 3.5 %collective-permute-done.26 = f32[12,4,10,1]{3,0,2,1:T(8,128)S(1)} collective-permute-done((f32[12,4,10,1]{3,0,2,1:T(8,128)S(1)}, f32[12,4,10,1]{3,0,2,1:T(8,128)S(1)}, u32[]{:S(2)}, u32[]{:S(2)}) %collective-permute-start.26) | collective-permute-done | bytes 1952 | tf_op jit(solution)/shard_map/ppermute | solution.py:42
  113.2 0.7 copy.464
  (196 shorter events, 16.9 us)
Async XLA Ops:
  0.6 53.9 %copy-start = (f32[12,12]{1,0:T(8,128)S(1)}, f32[12,12]{1,0:T(8,128)}, u32[]{:S(2)}) copy-start(f32[12,12]{1,0:T(8,128)} %param.17) | copy-start | bytes 1732
  1.5 12.9 %collective-permute-start = (f32[3,1,2,512]{3,2,1,0:T(2,128)S(1)}, f32[3,1,2,512]{3,2,1,0:T(2,128)S(1)}, u32[]{:S(2)}, u32[]{:S(2)}) collective-permute-start(f32[3,1,2,512]{3,2,1,0:T(2,128)S(1)} %get-tuple-element.118), channel_id=1, source_target_pairs={{0,1},{1,2},{2,3},{3,4},{4,5},{5,6},{6,7},{7,0},{8,9},{9,10},{10,1... | collective-permute-start | bytes 36872 | tf_op jit(solution)/shard_map/ppermute | solution.py:40
  2.0 12.4 %collective-permute-start.1 = (f32[3,1,2,512]{3,2,1,0:T(2,128)S(1)}, f32[3,1,2,512]{3,2,1,0:T(2,128)S(1)}, u32[]{:S(2)}, u32[]{:S(2)}) collective-permute-start(f32[3,1,2,512]{3,2,1,0:T(2,128)S(1)} %get-tuple-element.119), channel_id=1, source_target_pairs={{1,0},{2,1},{3,2},{4,3},{5,4},{6,5},{7,6},{0,7},{9,8},{10,9},{11,1... | collective-permute-start | bytes 36872 | tf_op jit(solution)/shard_map/ppermute | solution.py:42
  7.1 3.6 %copy-start.3 = (f32[1,8,512]{2,1,0:T(8,128)S(1)}, f32[1,8,512]{2,1,0:T(8,128)}, u32[]{:S(2)}) copy-start(f32[1,8,512]{2,1,0:T(8,128)} %param.10) | copy-start | bytes 49156
  7.2 17.6 %collective-permute-start.8 = (f32[12,4,1,128]{3,0,2,1:T(8,128)S(1)}, f32[12,4,1,128]{3,0,2,1:T(8,128)S(1)}, u32[]{:S(2)}, u32[]{:S(2)}) collective-permute-start(f32[12,4,1,128]{3,0,2,1:T(8,128)S(1)} %get-tuple-element.66), channel_id=1, source_target_pairs={{0,1},{1,2},{2,3},{3,4},{4,5},{5,6},{6,7},{7,0},{8,9},{9,10},{10,1... | collective-permute-start | bytes 73736 | tf_op jit(solution)/shard_map/ppermute | solution.py:40
  7.2 17.6 %collective-permute-start.9 = (f32[12,4,1,128]{3,0,2,1:T(8,128)S(1)}, f32[12,4,1,128]{3,0,2,1:T(8,128)S(1)}, u32[]{:S(2)}, u32[]{:S(2)}) collective-permute-start(f32[12,4,1,128]{3,0,2,1:T(8,128)S(1)} %get-tuple-element.67), channel_id=1, source_target_pairs={{1,0},{2,1},{3,2},{4,3},{5,4},{6,5},{7,6},{0,7},{9,8},{10,9},{11,1... | collective-permute-start | bytes 73736 | tf_op jit(solution)/shard_map/ppermute | solution.py:42
  10.8 0.7 copy-start.4
  11.6 0.7 copy-start.1
  12.4 0.7 copy-start.8
  13.1 1.3 %copy-start.7 = (f32[1,8,512]{2,1,0:T(8,128)S(1)}, f32[1,8,512]{2,1,0:T(8,128)}, u32[]{:S(2)}) copy-start(f32[1,8,512]{2,1,0:T(8,128)} %param.12) | copy-start | bytes 49156
  13.1 0.7 copy-start.11
  15.2 5.0 %collective-permute-start.2 = (f32[3,1,2,512]{3,2,1,0:T(2,128)S(1)}, f32[3,1,2,512]{3,2,1,0:T(2,128)S(1)}, u32[]{:S(2)}, u32[]{:S(2)}) collective-permute-start(f32[3,1,2,512]{3,2,1,0:T(2,128)S(1)} %get-tuple-element.116), channel_id=1, source_target_pairs={{0,1},{1,2},{2,3},{3,4},{4,5},{5,6},{6,7},{7,0},{8,9},{9,10},{10,1... | collective-permute-start | bytes 36872 | tf_op jit(solution)/shard_map/ppermute | solution.py:40
  15.3 4.9 %collective-permute-start.3 = (f32[3,1,2,512]{3,2,1,0:T(2,128)S(1)}, f32[3,1,2,512]{3,2,1,0:T(2,128)S(1)}, u32[]{:S(2)}, u32[]{:S(2)}) collective-permute-start(f32[3,1,2,512]{3,2,1,0:T(2,128)S(1)} %get-tuple-element.117), channel_id=1, source_target_pairs={{1,0},{2,1},{3,2},{4,3},{5,4},{6,5},{7,6},{0,7},{9,8},{10,9},{11,1... | collective-permute-start | bytes 36872 | tf_op jit(solution)/shard_map/ppermute | solution.py:42
  20.9 3.8 %copy-start.2 = (f32[12,4,8,128]{3,2,1,0:T(8,128)S(1)}, f32[12,4,8,128]{3,2,1,0:T(8,128)}, u32[]{:S(2)}) copy-start(f32[12,4,8,128]{3,2,1,0:T(8,128)} %param.16) | copy-start | bytes 589828
  21.1 8.3 %collective-permute-start.4 = (f32[3,1,2,512]{3,2,1,0:T(2,128)S(1)}, f32[3,1,2,512]{3,2,1,0:T(2,128)S(1)}, u32[]{:S(2)}, u32[]{:S(2)}) collective-permute-start(f32[3,1,2,512]{3,2,1,0:T(2,128)S(1)} %get-tuple-element.114), channel_id=1, source_target_pairs={{0,1},{1,2},{2,3},{3,4},{4,5},{5,6},{6,7},{7,0},{8,9},{9,10},{10,1... | collective-permute-start | bytes 36872 | tf_op jit(solution)/shard_map/ppermute | solution.py:40
  21.2 8.2 %collective-permute-start.5 = (f32[3,1,2,512]{3,2,1,0:T(2,128)S(1)}, f32[3,1,2,512]{3,2,1,0:T(2,128)S(1)}, u32[]{:S(2)}, u32[]{:S(2)}) collective-permute-start(f32[3,1,2,512]{3,2,1,0:T(2,128)S(1)} %get-tuple-element.115), channel_id=1, source_target_pairs={{1,0},{2,1},{3,2},{4,3},{5,4},{6,5},{7,6},{0,7},{9,8},{10,9},{11,1... | collective-permute-start | bytes 36872 | tf_op jit(solution)/shard_map/ppermute | solution.py:42
  24.9 0.6 copy-start.5
  26.4 26.9 %collective-permute-start.10 = (f32[12,4,10,1]{3,0,2,1:T(8,128)}, f32[12,4,10,1]{3,0,2,1:T(8,128)S(1)}, u32[]{:S(2)}, u32[]{:S(2)}) collective-permute-start(f32[12,4,10,1]{3,0,2,1:T(8,128)} %get-tuple-element.62), channel_id=1, source_target_pairs={{0,8},{8,16},{16,24},{24,0},{1,9},{9,17},{17,25},{25,1},{2,10},{10... | collective-permute-start | bytes 5768 | tf_op jit(solution)/shard_map/ppermute | solution.py:40
  28.4 24.9 %collective-permute-start.11 = (f32[12,4,10,1]{3,0,2,1:T(8,128)S(1)}, f32[12,4,10,1]{3,0,2,1:T(8,128)S(1)}, u32[]{:S(2)}, u32[]{:S(2)}) collective-permute-start(f32[12,4,10,1]{3,0,2,1:T(8,128)S(1)} %get-tuple-element.63), channel_id=1, source_target_pairs={{8,0},{16,8},{24,16},{0,24},{9,1},{17,9},{25,17},{1,25},{10,2},{18... | collective-permute-start | bytes 5768 | tf_op jit(solution)/shard_map/ppermute | solution.py:42
  30.1 5.0 %collective-permute-start.6 = (f32[3,1,2,512]{3,2,1,0:T(2,128)S(1)}, f32[3,1,2,512]{3,2,1,0:T(2,128)S(1)}, u32[]{:S(2)}, u32[]{:S(2)}) collective-permute-start(f32[3,1,2,512]{3,2,1,0:T(2,128)S(1)} %get-tuple-element.112), channel_id=1, source_target_pairs={{0,1},{1,2},{2,3},{3,4},{4,5},{5,6},{6,7},{7,0},{8,9},{9,10},{10,1... | collective-permute-start | bytes 36872 | tf_op jit(solution)/shard_map/ppermute | solution.py:40
  30.1 4.9 %collective-permute-start.7 = (f32[3,1,2,512]{3,2,1,0:T(2,128)S(1)}, f32[3,1,2,512]{3,2,1,0:T(2,128)S(1)}, u32[]{:S(2)}, u32[]{:S(2)}) collective-permute-start(f32[3,1,2,512]{3,2,1,0:T(2,128)S(1)} %get-tuple-element.113), channel_id=1, source_target_pairs={{1,0},{2,1},{3,2},{4,3},{5,4},{6,5},{7,6},{0,7},{9,8},{10,9},{11,1... | collective-permute-start | bytes 36872 | tf_op jit(solution)/shard_map/ppermute | solution.py:42
  42.3 8.1 %all-to-all-start = ((f32[4,1,3072]{2,1,0:T(1,128)}), f32[4,1,3072]{2,1,0:T(1,128)S(1)}, u32[]{:S(2)}, u32[]{:S(2)}) async-start(f32[4,1,3072]{2,1,0:T(1,128)} %reshape.1268), calls=%async_computation | async-start | bytes 98304 | tf_op jit(solution)/shard_map/all_to_all | solution.py:142
  53.2 0.8 copy-start.6
  54.5 0.7 copy-start.9
  55.4 0.7 copy-start.10
  56.2 3.7 %collective-permute-start.12 = (f32[1,8,128]{2,1,0:T(8,128)S(1)}, f32[1,8,128]{2,1,0:T(8,128)S(1)}, u32[]{:S(2)}, u32[]{:S(2)}) collective-permute-start(f32[1,8,128]{2,1,0:T(8,128)S(1)} %get-tuple-element.230), channel_id=1, source_target_pairs={{0,8},{8,0},{16,24},{24,16},{1,9},{9,1},{17,25},{25,17},{2,10},{10... | collective-permute-start | bytes 12296 | tf_op jit(solution)/shard_map/ppermute | solution.py:28
  57.0 3.6 %collective-permute-start.13 = (f32[1,8,128]{2,1,0:T(8,128)S(1)}, f32[1,8,128]{2,1,0:T(8,128)S(1)}, u32[]{:S(2)}, u32[]{:S(2)}) collective-permute-start(f32[1,8,128]{2,1,0:T(8,128)S(1)} %get-tuple-element.229), channel_id=1, source_target_pairs={{0,16},{8,24},{16,0},{24,8},{1,17},{9,25},{17,1},{25,9},{2,18},{10... | collective-permute-start | bytes 12296 | tf_op jit(solution)/shard_map/ppermute | solution.py:28
  57.4 4.5 %collective-permute-start.14 = (f32[1,8,128]{2,1,0:T(8,128)S(1)}, f32[1,8,128]{2,1,0:T(8,128)S(1)}, u32[]{:S(2)}, u32[]{:S(2)}) collective-permute-start(f32[1,8,128]{2,1,0:T(8,128)S(1)} %get-tuple-element.228), channel_id=1, source_target_pairs={{0,24},{8,16},{16,8},{24,0},{1,25},{9,17},{17,9},{25,1},{2,26},{10... | collective-permute-start | bytes 12296 | tf_op jit(solution)/shard_map/ppermute | solution.py:28
  62.0 7.2 %collective-permute-start.15 = (f32[3,1,2,512]{3,2,1,0:T(2,128)S(1)}, f32[3,1,2,512]{3,2,1,0:T(2,128)S(1)}, u32[]{:S(2)}, u32[]{:S(2)}) collective-permute-start(f32[3,1,2,512]{3,2,1,0:T(2,128)S(1)} %get-tuple-element.104), channel_id=1, source_target_pairs={{0,1},{1,2},{2,3},{3,4},{4,5},{5,6},{6,7},{7,0},{8,9},{9,10},{10,1... | collective-permute-start | bytes 36872 | tf_op jit(solution)/shard_map/ppermute | solution.py:40
  62.0 7.1 %collective-permute-start.16 = (f32[3,1,2,512]{3,2,1,0:T(2,128)S(1)}, f32[3,1,2,512]{3,2,1,0:T(2,128)S(1)}, u32[]{:S(2)}, u32[]{:S(2)}) collective-permute-start(f32[3,1,2,512]{3,2,1,0:T(2,128)S(1)} %get-tuple-element.105), channel_id=1, source_target_pairs={{1,0},{2,1},{3,2},{4,3},{5,4},{6,5},{7,6},{0,7},{9,8},{10,9},{11,1... | collective-permute-start | bytes 36872 | tf_op jit(solution)/shard_map/ppermute | solution.py:42
  65.6 8.1 %collective-permute-start.23 = (f32[12,4,1,128]{3,0,2,1:T(8,128)S(1)}, f32[12,4,1,128]{3,0,2,1:T(8,128)S(1)}, u32[]{:S(2)}, u32[]{:S(2)}) collective-permute-start(f32[12,4,1,128]{3,0,2,1:T(8,128)S(1)} %get-tuple-element.64), channel_id=1, source_target_pairs={{0,1},{1,2},{2,3},{3,4},{4,5},{5,6},{6,7},{7,0},{8,9},{9,10},{10,1... | collective-permute-start | bytes 73736 | tf_op jit(solution)/shard_map/ppermute | solution.py:40
  65.6 8.1 %collective-permute-start.24 = (f32[12,4,1,128]{3,0,2,1:T(8,128)S(1)}, f32[12,4,1,128]{3,0,2,1:T(8,128)S(1)}, u32[]{:S(2)}, u32[]{:S(2)}) collective-permute-start(f32[12,4,1,128]{3,0,2,1:T(8,128)S(1)} %get-tuple-element.65), channel_id=1, source_target_pairs={{1,0},{2,1},{3,2},{4,3},{5,4},{6,5},{7,6},{0,7},{9,8},{10,9},{11,1... | collective-permute-start | bytes 73736 | tf_op jit(solution)/shard_map/ppermute | solution.py:42
  70.0 5.0 %collective-permute-start.17 = (f32[3,1,2,512]{3,2,1,0:T(2,128)S(1)}, f32[3,1,2,512]{3,2,1,0:T(2,128)S(1)}, u32[]{:S(2)}, u32[]{:S(2)}) collective-permute-start(f32[3,1,2,512]{3,2,1,0:T(2,128)S(1)} %get-tuple-element.102), channel_id=1, source_target_pairs={{0,1},{1,2},{2,3},{3,4},{4,5},{5,6},{6,7},{7,0},{8,9},{9,10},{10,1... | collective-permute-start | bytes 36872 | tf_op jit(solution)/shard_map/ppermute | solution.py:40
  70.1 4.9 %collective-permute-start.18 = (f32[3,1,2,512]{3,2,1,0:T(2,128)S(1)}, f32[3,1,2,512]{3,2,1,0:T(2,128)S(1)}, u32[]{:S(2)}, u32[]{:S(2)}) collective-permute-start(f32[3,1,2,512]{3,2,1,0:T(2,128)S(1)} %get-tuple-element.103), channel_id=1, source_target_pairs={{1,0},{2,1},{3,2},{4,3},{5,4},{6,5},{7,6},{0,7},{9,8},{10,9},{11,1... | collective-permute-start | bytes 36872 | tf_op jit(solution)/shard_map/ppermute | solution.py:42
  75.9 5.0 %collective-permute-start.19 = (f32[3,1,2,512]{3,2,1,0:T(2,128)S(1)}, f32[3,1,2,512]{3,2,1,0:T(2,128)S(1)}, u32[]{:S(2)}, u32[]{:S(2)}) collective-permute-start(f32[3,1,2,512]{3,2,1,0:T(2,128)S(1)} %get-tuple-element.100), channel_id=1, source_target_pairs={{0,1},{1,2},{2,3},{3,4},{4,5},{5,6},{6,7},{7,0},{8,9},{9,10},{10,1... | collective-permute-start | bytes 36872 | tf_op jit(solution)/shard_map/ppermute | solution.py:40
  76.0 5.0 %collective-permute-start.20 = (f32[3,1,2,512]{3,2,1,0:T(2,128)S(1)}, f32[3,1,2,512]{3,2,1,0:T(2,128)S(1)}, u32[]{:S(2)}, u32[]{:S(2)}) collective-permute-start(f32[3,1,2,512]{3,2,1,0:T(2,128)S(1)} %get-tuple-element.101), channel_id=1, source_target_pairs={{1,0},{2,1},{3,2},{4,3},{5,4},{6,5},{7,6},{0,7},{9,8},{10,9},{11,1... | collective-permute-start | bytes 36872 | tf_op jit(solution)/shard_map/ppermute | solution.py:42
  81.8 5.0 %collective-permute-start.21 = (f32[3,1,2,512]{3,2,1,0:T(2,128)S(1)}, f32[3,1,2,512]{3,2,1,0:T(2,128)S(1)}, u32[]{:S(2)}, u32[]{:S(2)}) collective-permute-start(f32[3,1,2,512]{3,2,1,0:T(2,128)S(1)} %get-tuple-element.98), channel_id=1, source_target_pairs={{0,1},{1,2},{2,3},{3,4},{4,5},{5,6},{6,7},{7,0},{8,9},{9,10},{10,1... | collective-permute-start | bytes 36872 | tf_op jit(solution)/shard_map/ppermute | solution.py:40
  81.9 5.2 %collective-permute-start.22 = (f32[3,1,2,512]{3,2,1,0:T(2,128)S(1)}, f32[3,1,2,512]{3,2,1,0:T(2,128)S(1)}, u32[]{:S(2)}, u32[]{:S(2)}) collective-permute-start(f32[3,1,2,512]{3,2,1,0:T(2,128)S(1)} %get-tuple-element.99), channel_id=1, source_target_pairs={{1,0},{2,1},{3,2},{4,3},{5,4},{6,5},{7,6},{0,7},{9,8},{10,9},{11,1... | collective-permute-start | bytes 36872 | tf_op jit(solution)/shard_map/ppermute | solution.py:42
  94.2 8.6 %all-to-all-start.1 = ((f32[4,1,3072]{2,1,0:T(1,128)}), f32[4,1,3072]{2,1,0:T(1,128)S(1)}, u32[]{:S(2)}, u32[]{:S(2)}) async-start(f32[4,1,3072]{2,1,0:T(1,128)} %reshape.1270), calls=%async_computation.1 | async-start | bytes 98304 | tf_op jit(solution)/shard_map/all_to_all | solution.py:142
  98.0 10.7 %collective-permute-start.25 = (f32[12,4,10,1]{3,0,2,1:T(8,128)S(1)}, f32[12,4,10,1]{3,0,2,1:T(8,128)S(1)}, u32[]{:S(2)}, u32[]{:S(2)}) collective-permute-start(f32[12,4,10,1]{3,0,2,1:T(8,128)S(1)} %get-tuple-element.60), channel_id=1, source_target_pairs={{0,8},{8,16},{16,24},{24,0},{1,9},{9,17},{17,25},{25,1},{2,10},{10... | collective-permute-start | bytes 5768 | tf_op jit(solution)/shard_map/ppermute | solution.py:40
  100.1 12.2 %collective-permute-start.26 = (f32[12,4,10,1]{3,0,2,1:T(8,128)S(1)}, f32[12,4,10,1]{3,0,2,1:T(8,128)S(1)}, u32[]{:S(2)}, u32[]{:S(2)}) collective-permute-start(f32[12,4,10,1]{3,0,2,1:T(8,128)S(1)} %get-tuple-element.61), channel_id=1, source_target_pairs={{8,0},{16,8},{24,16},{0,24},{9,1},{17,9},{25,17},{1,25},{10,2},{18... | collective-permute-start | bytes 5768 | tf_op jit(solution)/shard_map/ppermute | solution.py:42
